TPU v7x, 256 devices: a whole 4x4x8 slice. The times are simulated.
256 devices in a mesh: seq: 32 (over y, z), grp: 8 (over x, core).
Axes of the slice: x: 4, y: 4, z: 8, core: 2. Of those that a mesh axis runs over, the one named last changes fastest.
Arguments:
- mixer_input: bfloat16 [5120, 32768], P('grp', 'seq'), may hold values from -5 to 5
- step_sizes: float32 [80, 32768], P('grp', 'seq'), may hold values from 0 to 1, as said below
- decay_rates: float32 [80], P('grp'), may hold values from 1 to 2
- skip_gain: float32 [80], P('grp'), may hold values from 0.5 to 1.5
- input_basis: bfloat16 [32768, 128], P('seq'), may hold values from -5 to 5
- output_basis: bfloat16 [32768, 128], P('seq'), may hold values from -0.5 to 0.5
- out_weight: bfloat16 [5120, 2560], P(None, 'grp'), may hold values from -0.078125 to 0.078125
Outputs:
- layer_output: bfloat16 [32768, 2560], P('seq', 'grp')
Inputs may be any that keep to these rules, and one draw needn't show every extreme that they name: `step_sizes`: positive step sizes.
All inputs are finite; a program needn't handle non-finite values.
Results may differ from a plain program's by a relative error of at most 0.0065.
Values may be sent and summed in bfloat16 or wider, within the bound.
A program may use at most 128 MiB of HBM per device.

v0:
```python
import jax
import jax.numpy as jnp
from jax import lax
from jax.sharding import PartitionSpec as P

HP = 64
N = 128
GROUP = 256


def carry_in(total_log, final_state):
    peers, here = (lax.axis_size("seq"), lax.axis_index("seq"))

    def shifted(value, d):
        return lax.ppermute(value, "seq", [(i, i + d) for i in range(peers - d)])

    decay = shifted(jnp.exp(total_log), 1)
    decay = jnp.where(here >= 1, decay, jnp.ones_like(decay))
    state = shifted(final_state, 1)
    d = 1
    while d < peers:
        decay_r, state_r = (shifted(decay, d), shifted(state, d))
        reached = here >= d
        state = jnp.where(reached, decay[:, None, None] * state_r + state, state)
        decay = jnp.where(reached, decay * decay_r, decay)
        d *= 2
    return state


def on_device(
    mixer_input, step_sizes, decay_rates, skip_gain, input_basis, output_basis, out_weight
):
    heads_here = step_sizes.shape[0]
    tokens_here = step_sizes.shape[1]
    count = tokens_here // GROUP
    channels = mixer_input.reshape(heads_here, HP, count, GROUP)
    log_decay = -(decay_rates[:, None] * step_sizes).reshape(heads_here, count, GROUP)
    steps_blocked = step_sizes.reshape(heads_here, count, GROUP)
    running = jnp.cumsum(log_decay, axis=2)
    basis_in_blocked = input_basis.reshape(count, GROUP, N)
    basis_out_blocked = output_basis.reshape(count, GROUP, N)
    gram = jnp.einsum(
        "cin,cjn->cij", basis_out_blocked, basis_in_blocked, preferred_element_type=jnp.float32
    )
    rows_index = lax.broadcasted_iota(jnp.int32, (GROUP, GROUP), 0)
    cols_index = lax.broadcasted_iota(jnp.int32, (GROUP, GROUP), 1)
    causal = rows_index >= cols_index
    gaps = running[:, :, :, None] - running[:, :, None, :]
    mixing = jnp.where(
        causal,
        gram[None] * jnp.exp(jnp.where(causal, gaps, 0.0)) * steps_blocked[:, :, None, :],
        0.0,
    ).astype(jnp.bfloat16)
    inner = jnp.einsum("hcij,hpcj->hpci", mixing, channels, preferred_element_type=jnp.float32)
    tail = jnp.exp(running[:, :, -1:] - running) * steps_blocked
    weighted_terms = (basis_in_blocked.astype(jnp.float32)[None] * tail[:, :, :, None]).astype(
        jnp.bfloat16
    )
    summaries = jnp.einsum(
        "hcjn,hpcj->chnp", weighted_terms, channels, preferred_element_type=jnp.float32
    )
    block_decay = jnp.exp(running[:, :, -1])

    def advance(state, pair):
        decay, digest_record = pair
        return (decay[:, None, None] * state + digest_record, state)

    zero_state = jnp.zeros((heads_here, N, HP), jnp.float32)
    final_state, entering = lax.scan(advance, zero_state, (block_decay.T, summaries))
    block_sums = jnp.sum(log_decay, axis=2)
    prefix = jnp.exp(jnp.cumsum(block_sums, axis=1) - block_sums)
    total_log = jnp.sum(block_sums, axis=1)
    basis_out_wide = basis_out_blocked.astype(jnp.float32)
    within = jnp.exp(running)[:, None]
    direct = skip_gain[:, None, None, None] * channels.astype(jnp.float32)
    carried = carry_in(total_log, final_state)
    states = entering + prefix.T[:, :, None, None] * carried[None]
    from_state = jnp.einsum(
        "cin,chnp->hpci", basis_out_wide, states, precision=lax.Precision.HIGHEST
    )
    mixed = inner + from_state * within + direct
    mixed_columns = mixed.astype(jnp.bfloat16).reshape(heads_here * HP, tokens_here)
    result = jnp.einsum(
        "kt,kd->td",
        lax.all_gather(mixed_columns, "grp", axis=0, tiled=True),
        out_weight,
        preferred_element_type=jnp.float32,
    )
    return result.astype(jnp.bfloat16)


def solution(mesh):
    placed = (
        P("grp", "seq"),
        P("grp", "seq"),
        P("grp"),
        P("grp"),
        P("seq", None),
        P("seq", None),
        P(None, "grp"),
    )
    return jax.shard_map(
        on_device, mesh=mesh, in_specs=placed, out_specs=P("seq", "grp"), check_vma=False
    )
```

profile of v0, /device:TPU:1, one launch (start us, length us, event | category | flops | bytes accessed | tf_op | source)
XLA Modules:
  0.0 231.2 jit_solution(14767401530149646596)
XLA Ops:
  6.5 1.0 mul.141
  7.6 1.0 fusion.19
  9.3 2.3 reduce-window.6
  12.9 1.8 convert_element_type.24
  14.7 3.8 %reshape.94 = bf16[10,64,4,256]{3,2,1,0:T(4,128)(2,1)} reshape(bf16[640,1024]{1,0:T(8,128)(2,1)} %param.9) | data formatting | bytes 2621440 | tf_op jit(solution)/shard_map/reshape | solution.py:36
  18.5 5.6 %fusion.8 = f32[4,10,128,64]{3,2,1,0:T(8,128)} fusion(f32[10,4,256]{2,0,1:T(8,128)S(1)} %copy.35, f32[4,256,128]{2,1,0:T(8,128)} %convert_element_type.24, bf16[10,64,4,256]{3,2,1,0:T(4,128)(2,1)} %reshape.94), kind=kOutput, calls=%fused_computation.13 | convolution fusion | flops 170393600 | bytes 3186688 | tf_op jit(solution)/shard_map/hcjn,hpcj->chnp/dot_general | solution.py:59
  24.1 15.7 %while.13 = (s32[]{:T(128)}, f32[10,128,64]{2,1,0:T(8,128)}, f32[4,10,128,64]{3,2,1,0:T(8,128)}, f32[4,10]{1,0:T(4,128)S(1)}, f32[4,10,128,64]{3,2,1,0:T(8,128)}, /*index=5*/s32[]{:T(128)}, s32[]{:T(128)}) while((s32[]{:T(128)}, f32[10,128,64]{2,1,0:T(8,128)}, f32[4,10,128,64]{3,2,1,0:T(8,128)}, f32[4,10]{1,0:T(4,128)S(1)}, ...), condition=%wide.region_3.4_spmd.clone, body=%wide.region_2.3_spmd.clone.sunk | while | flops 327683 | bytes 2293988 | solution.py:69
  24.1 0.9 bitcast_dynamic-update-slice_fusion.2
  25.1 2.1 bitcast_add_fusion.2
  27.1 2.0 bitcast_dynamic-update-slice_fusion.2
  29.1 2.3 bitcast_add_fusion.2
  31.4 2.0 bitcast_dynamic-update-slice_fusion.2
  33.4 2.3 bitcast_add_fusion.2
  35.6 2.0 bitcast_dynamic-update-slice_fusion.2
  37.6 2.3 bitcast_add_fusion.2
  39.9 2.1 copy.39
  41.9 5.1 %collective-permute-start.5 = (f32[10,128,64]{1,2,0:T(8,128)}, f32[10,128,64]{1,2,0:T(8,128)}, u32[]{:S(2)}, u32[]{:S(2)}) collective-permute-start(f32[10,128,64]{1,2,0:T(8,128)} %copy.39), channel_id=1, source_target_pairs={{0,8},{8,16},{16,24},{24,32},{32,40},{40,48},{48,56},{56,64},{64,7... | collective-permute-start | bytes 983048 | tf_op jit(solution)/shard_map/ppermute | solution.py:15
  47.0 6.0 %collective-permute-done.5 = f32[10,128,64]{1,2,0:T(8,128)} collective-permute-done((f32[10,128,64]{1,2,0:T(8,128)}, f32[10,128,64]{1,2,0:T(8,128)}, u32[]{:S(2)}, u32[]{:S(2)}) %collective-permute-start.5) | collective-permute-done | bytes 327712 | tf_op jit(solution)/shard_map/ppermute | solution.py:15
  53.0 4.8 %collective-permute-start.6 = (f32[10,128,64]{1,2,0:T(8,128)}, f32[10,128,64]{1,2,0:T(8,128)}, u32[]{:S(2)}, u32[]{:S(2)}) collective-permute-start(f32[10,128,64]{1,2,0:T(8,128)} %collective-permute-done.5), channel_id=1, source_target_pairs={{0,8},{8,16},{16,24},{24,32},{32,40},{40,48},{48,56},{56,64},{64,7... | collective-permute-start | bytes 983048 | tf_op jit(solution)/shard_map/ppermute | solution.py:15
  57.8 2.8 %collective-permute-start = (f32[10]{0:T(128)S(1)}, f32[10]{0:T(128)S(1)}, u32[]{:S(2)}, u32[]{:S(2)}) collective-permute-start(f32[10]{0:T(128)S(1)} %negate_exponential_fusion), channel_id=1, source_target_pairs={{0,8},{8,16},{16,24},{24,32},{32,40},{40,48},{48,56},{56,64},{64,7... | collective-permute-start | bytes 128 | tf_op jit(solution)/shard_map/ppermute | solution.py:15
  60.7 2.2 collective-permute-done
  62.9 1.9 add_select_fusion.4
  64.8 6.6 %collective-permute-start.7 = (f32[10,128,64]{1,2,0:T(8,128)}, f32[10,128,64]{1,2,0:T(8,128)}, u32[]{:S(2)}, u32[]{:S(2)}) collective-permute-start(f32[10,128,64]{1,2,0:T(8,128)} %add_select_fusion.4), channel_id=1, source_target_pairs={{0,16},{8,24},{16,32},{24,40},{32,48},{40,56},{48,64},{56,72},{64,... | collective-permute-start | bytes 983048 | tf_op jit(solution)/shard_map/ppermute | solution.py:15
  71.3 5.0 %collective-permute-start.1 = (f32[10]{0:T(128)S(1)}, f32[10]{0:T(128)S(1)}, u32[]{:S(2)}, u32[]{:S(2)}) collective-permute-start(f32[10]{0:T(128)S(1)} %broadcast_select_fusion.1), channel_id=1, source_target_pairs={{0,8},{8,16},{16,24},{24,32},{32,40},{40,48},{48,56},{56,64},{64,7... | collective-permute-start | bytes 128 | tf_op jit(solution)/shard_map/ppermute | solution.py:15
  77.0 1.9 add_select_fusion.3
  79.0 20.3 %collective-permute-start.8 = (f32[10,128,64]{1,2,0:T(8,128)}, f32[10,128,64]{1,2,0:T(8,128)}, u32[]{:S(2)}, u32[]{:S(2)}) collective-permute-start(f32[10,128,64]{1,2,0:T(8,128)} %add_select_fusion.3), channel_id=1, source_target_pairs={{0,32},{8,40},{16,48},{24,56},{32,64},{40,72},{48,80},{56,88},{64,... | collective-permute-start | bytes 983048 | tf_op jit(solution)/shard_map/ppermute | solution.py:15
  99.3 2.2 fusion.22
  101.5 1.5 reshape.95
  103.0 0.9 reduce_sum.18
  103.9 0.8 reduce_window_sum.43
  104.7 1.3 collective-permute-start.2
  106.0 7.2 %collective-permute-done.2 = f32[10]{0:T(128)S(1)} collective-permute-done((f32[10]{0:T(128)}, f32[10]{0:T(128)S(1)}, u32[]{:S(2)}, u32[]{:S(2)}) %collective-permute-start.2) | collective-permute-done | bytes 72 | tf_op jit(solution)/shard_map/ppermute | solution.py:15
  113.8 1.9 add_select_fusion.2
  115.7 5.6 %collective-permute-start.9 = (f32[10,128,64]{1,2,0:T(8,128)}, f32[10,128,64]{1,2,0:T(8,128)}, u32[]{:S(2)}, u32[]{:S(2)}) collective-permute-start(f32[10,128,64]{1,2,0:T(8,128)} %add_select_fusion.2), channel_id=1, source_target_pairs={{0,64},{8,72},{16,80},{24,88},{32,96},{40,104},{48,112},{56,120},{... | collective-permute-start | bytes 983048 | tf_op jit(solution)/shard_map/ppermute | solution.py:15
  122.1 3.8 %collective-permute-start.3 = (f32[10]{0:T(128)}, f32[10]{0:T(128)S(1)}, u32[]{:S(2)}, u32[]{:S(2)}) collective-permute-start(f32[10]{0:T(128)} %copy-done.13), channel_id=1, source_target_pairs={{0,32},{8,40},{16,48},{24,56},{32,64},{40,72},{48,80},{56,88},{64,... | collective-permute-start | bytes 128 | tf_op jit(solution)/shard_map/ppermute | solution.py:15
  125.9 0.9 collective-permute-done.3
  127.5 1.2 add_select_fusion.1
  128.7 8.7 %collective-permute-start.10 = (f32[10,128,64]{1,2,0:T(8,128)S(1)}, f32[10,128,64]{1,2,0:T(8,128)S(1)}, u32[]{:S(2)}, u32[]{:S(2)}) collective-permute-start(f32[10,128,64]{1,2,0:T(8,128)S(1)} %add_select_fusion.1), channel_id=1, source_target_pairs={{0,128},{8,136},{16,144},{24,152},{32,160},{40,168},{48,176},{56,1... | collective-permute-start | bytes 983048 | tf_op jit(solution)/shard_map/ppermute | solution.py:15
  138.0 1.3 collective-permute-start.4
  139.3 3.3 %collective-permute-done.4 = f32[10]{0:T(128)S(1)} collective-permute-done((f32[10]{0:T(128)S(1)}, f32[10]{0:T(128)S(1)}, u32[]{:S(2)}, u32[]{:S(2)}) %collective-permute-start.4) | collective-permute-done | bytes 72 | tf_op jit(solution)/shard_map/ppermute | solution.py:15
  142.6 0.8 add_select_fusion
  143.5 2.0 copy.40
  145.6 4.4 %fusion.12 = f32[4,10,64,256]{3,2,0,1:T(8,128)S(1)} fusion(bf16[4,256,128,1]{2,1,0,3:T(8,128)(2,1)S(1)} %bitcast.46, f32[4,10,128,64]{3,2,1,0:T(8,128)} %get-tuple-element.33, f32[10,128,64]{2,1,0:T(8,128)} %copy.40, f32[4,10]{1,0:T(4,128)S(1)} %copy.38), kind=kOutput, calls=%fused_computation.18 | convolution fusion | flops 1007288320 | bytes 4522144 | tf_op jit(solution)/shard_map/cin,chnp->hpci/dot_general | solution.py:78
  150.0 4.0 %fusion.11 = bf16[10,64,4,256]{3,1,2,0:T(8,128)(2,1)S(1)} fusion(f32[4,10,64,256]{3,2,0,1:T(8,128)S(1)} %fusion.12, f32[10,4,256]{2,1,0:T(4,128)S(1)} %copy-done.9, f32[10,4,256]{2,1,0:T(4,128)S(1)} %copy-done.7, f32[4,256,256]{2,1,0:T(8,128)S(1)} %copy-done.2, pred[256,256]{1,0:T(8,128)(4,1)S(1)} %copy-done.10, bf16[10,64,4,256]{3,2,1,0:T(4,128)(2,1)S(1)} %copy-done.1, ...), kind=kOutput, calls=%fused_computation.17 | convolution fusion | flops 355205120 | bytes 6479912 | tf_op jit(solution)/shard_map/hcij,hpcj->hpci/dot_general | solution.py:54
  154.0 1.0 copy.43
  155.0 1.4 copy.47
  156.4 60.8 %all-gather.2.cloned.1.call-done = bf16[5120,1024]{1,0:T(8,128)(2,1)} async-done(((bf16[640,1024]{1,0:T(8,128)(2,1)}), bf16[5120,1024]{1,0:T(8,128)(2,1)}) %all-gather.2.cloned.1.call-update) | async-done | bytes 10485776 | tf_op jit(solution)/shard_map/all_gather | solution.py:85
  217.2 7.2 %convolution_convert_fusion = bf16[1024,320]{0,1:T(8,128)(2,1)} fusion(bf16[5120,320]{0,1:T(8,128)(2,1)S(1)} %copy-done, bf16[5120,1024]{1,0:T(8,128)(2,1)} %all-gather.2.cloned.1.call-done), kind=kOutput, calls=%fused_computation.23 | convolution fusion | flops 3355770880 | bytes 14417920 | tf_op jit(solution)/shard_map/kt,kd->td/dot_general | solution.py:83
  (69 shorter events, 5.6 us)
Async XLA Ops:
  6.5 210.6 %copy-start = (bf16[5120,320]{0,1:T(8,128)(2,1)S(1)}, bf16[5120,320]{0,1:T(8,128)(2,1)}, u32[]{:S(2)}) copy-start(bf16[5120,320]{0,1:T(8,128)(2,1)} %param.15) | copy-start | bytes 9830404
  6.5 210.6 %all-gather.2.cloned.1.call-start = ((), (), s32[]{:S(2)}) async-start(), calls=%async_computation | async-start | bytes 11796480 | tf_op jit(solution)/shard_map/all_gather | solution.py:85
  7.6 16.6 %copy-start.8 = (f32[10,4,256]{2,1,0:T(4,128)}, f32[10,4,256]{2,1,0:T(4,128)S(1)}, u32[]{:S(2)}) copy-start(f32[10,4,256]{2,1,0:T(4,128)S(1)} %mul.141) | copy-start | bytes 122884
  8.6 0.6 copy-start.5
  12.0 12.1 %copy-start.6 = (f32[10,4,256]{2,1,0:T(4,128)}, f32[10,4,256]{2,1,0:T(4,128)S(1)}, u32[]{:S(2)}) copy-start(f32[10,4,256]{2,1,0:T(4,128)S(1)} %reduce_window_sum.42) | copy-start | bytes 122884
  39.9 59.4 %copy-start.3 = (bf16[1024,128]{1,0:T(8,128)(2,1)S(1)}, bf16[1024,128]{1,0:T(8,128)(2,1)}, u32[]{:S(2)}) copy-start(bf16[1024,128]{1,0:T(8,128)(2,1)} %param.13) | copy-start | bytes 786436
  41.9 11.0 %collective-permute-start.5 = (f32[10,128,64]{1,2,0:T(8,128)}, f32[10,128,64]{1,2,0:T(8,128)}, u32[]{:S(2)}, u32[]{:S(2)}) collective-permute-start(f32[10,128,64]{1,2,0:T(8,128)} %copy.39), channel_id=1, source_target_pairs={{0,8},{8,16},{16,24},{24,32},{32,40},{40,48},{48,56},{56,64},{64,7... | collective-permute-start | bytes 983048 | tf_op jit(solution)/shard_map/ppermute | solution.py:15
  53.0 9.9 %collective-permute-start.6 = (f32[10,128,64]{1,2,0:T(8,128)}, f32[10,128,64]{1,2,0:T(8,128)}, u32[]{:S(2)}, u32[]{:S(2)}) collective-permute-start(f32[10,128,64]{1,2,0:T(8,128)} %collective-permute-done.5), channel_id=1, source_target_pairs={{0,8},{8,16},{16,24},{24,32},{32,40},{40,48},{48,56},{56,64},{64,7... | collective-permute-start | bytes 983048 | tf_op jit(solution)/shard_map/ppermute | solution.py:15
  57.8 5.0 %collective-permute-start = (f32[10]{0:T(128)S(1)}, f32[10]{0:T(128)S(1)}, u32[]{:S(2)}, u32[]{:S(2)}) collective-permute-start(f32[10]{0:T(128)S(1)} %negate_exponential_fusion), channel_id=1, source_target_pairs={{0,8},{8,16},{16,24},{24,32},{32,40},{40,48},{48,56},{56,64},{64,7... | collective-permute-start | bytes 128 | tf_op jit(solution)/shard_map/ppermute | solution.py:15
  64.8 12.3 %collective-permute-start.7 = (f32[10,128,64]{1,2,0:T(8,128)}, f32[10,128,64]{1,2,0:T(8,128)}, u32[]{:S(2)}, u32[]{:S(2)}) collective-permute-start(f32[10,128,64]{1,2,0:T(8,128)} %add_select_fusion.4), channel_id=1, source_target_pairs={{0,16},{8,24},{16,32},{24,40},{32,48},{40,56},{48,64},{56,72},{64,... | collective-permute-start | bytes 983048 | tf_op jit(solution)/shard_map/ppermute | solution.py:15
  71.3 5.7 %collective-permute-start.1 = (f32[10]{0:T(128)S(1)}, f32[10]{0:T(128)S(1)}, u32[]{:S(2)}, u32[]{:S(2)}) collective-permute-start(f32[10]{0:T(128)S(1)} %broadcast_select_fusion.1), channel_id=1, source_target_pairs={{0,8},{8,16},{16,24},{24,32},{32,40},{40,48},{48,56},{56,64},{64,7... | collective-permute-start | bytes 128 | tf_op jit(solution)/shard_map/ppermute | solution.py:15
  77.0 22.3 %copy-start.12 = (f32[10]{0:T(128)}, f32[10]{0:T(128)S(1)}, u32[]{:S(2)}) copy-start(f32[10]{0:T(128)S(1)} %broadcast_select_fusion) | copy-start | bytes 124
  79.0 34.9 %collective-permute-start.8 = (f32[10,128,64]{1,2,0:T(8,128)}, f32[10,128,64]{1,2,0:T(8,128)}, u32[]{:S(2)}, u32[]{:S(2)}) collective-permute-start(f32[10,128,64]{1,2,0:T(8,128)} %add_select_fusion.3), channel_id=1, source_target_pairs={{0,32},{8,40},{16,48},{24,56},{32,64},{40,72},{48,80},{56,88},{64,... | collective-permute-start | bytes 983048 | tf_op jit(solution)/shard_map/ppermute | solution.py:15
  101.5 44.0 %copy-start.4 = (bf16[1024,128]{1,0:T(8,128)(2,1)S(1)}, bf16[1024,128]{1,0:T(8,128)(2,1)}, u32[]{:S(2)}) copy-start(bf16[1024,128]{1,0:T(8,128)(2,1)} %param.14) | copy-start | bytes 786436
  104.7 8.5 %collective-permute-start.2 = (f32[10]{0:T(128)}, f32[10]{0:T(128)S(1)}, u32[]{:S(2)}, u32[]{:S(2)}) collective-permute-start(f32[10]{0:T(128)} %copy-done.12), channel_id=1, source_target_pairs={{0,16},{8,24},{16,32},{24,40},{32,48},{40,56},{48,64},{56,72},{64,... | collective-permute-start | bytes 128 | tf_op jit(solution)/shard_map/ppermute | solution.py:15
  113.8 1.9 copy-start.13
  115.7 11.8 %collective-permute-start.9 = (f32[10,128,64]{1,2,0:T(8,128)}, f32[10,128,64]{1,2,0:T(8,128)}, u32[]{:S(2)}, u32[]{:S(2)}) collective-permute-start(f32[10,128,64]{1,2,0:T(8,128)} %add_select_fusion.2), channel_id=1, source_target_pairs={{0,64},{8,72},{16,80},{24,88},{32,96},{40,104},{48,112},{56,120},{... | collective-permute-start | bytes 983048 | tf_op jit(solution)/shard_map/ppermute | solution.py:15
  122.1 4.7 %collective-permute-start.3 = (f32[10]{0:T(128)}, f32[10]{0:T(128)S(1)}, u32[]{:S(2)}, u32[]{:S(2)}) collective-permute-start(f32[10]{0:T(128)} %copy-done.13), channel_id=1, source_target_pairs={{0,32},{8,40},{16,48},{24,56},{32,64},{40,72},{48,80},{56,88},{64,... | collective-permute-start | bytes 128 | tf_op jit(solution)/shard_map/ppermute | solution.py:15
  128.7 13.9 %collective-permute-start.10 = (f32[10,128,64]{1,2,0:T(8,128)S(1)}, f32[10,128,64]{1,2,0:T(8,128)S(1)}, u32[]{:S(2)}, u32[]{:S(2)}) collective-permute-start(f32[10,128,64]{1,2,0:T(8,128)S(1)} %add_select_fusion.1), channel_id=1, source_target_pairs={{0,128},{8,136},{16,144},{24,152},{32,160},{40,168},{48,176},{56,1... | collective-permute-start | bytes 983048 | tf_op jit(solution)/shard_map/ppermute | solution.py:15
  138.0 4.6 %collective-permute-start.4 = (f32[10]{0:T(128)S(1)}, f32[10]{0:T(128)S(1)}, u32[]{:S(2)}, u32[]{:S(2)}) collective-permute-start(f32[10]{0:T(128)S(1)} %broadcast_select_fusion.3), channel_id=1, source_target_pairs={{0,64},{8,72},{16,80},{24,88},{32,96},{40,104},{48,112},{56,120},{... | collective-permute-start | bytes 128 | tf_op jit(solution)/shard_map/ppermute | solution.py:15
  145.5 4.4 %copy-start.1 = (bf16[10,64,4,256]{3,2,1,0:T(4,128)(2,1)S(1)}, bf16[10,64,4,256]{3,2,1,0:T(4,128)(2,1)}, u32[]{:S(2)}) copy-start(bf16[10,64,4,256]{3,2,1,0:T(4,128)(2,1)} %reshape.94) | copy-start | bytes 3932164
  145.5 4.4 %copy-start.2 = (f32[4,256,256]{2,1,0:T(8,128)S(1)}, f32[4,256,256]{2,1,0:T(8,128)}, u32[]{:S(2)}) copy-start(f32[4,256,256]{2,1,0:T(8,128)} %fusion.22) | copy-start | bytes 3145732
  145.5 4.5 %copy-start.7 = (f32[10,4,256]{2,1,0:T(4,128)S(1)}, f32[10,4,256]{2,1,0:T(4,128)}, u32[]{:S(2)}) copy-start(f32[10,4,256]{2,1,0:T(4,128)} %copy-done.6) | copy-start | bytes 122884
  145.5 4.5 %copy-start.9 = (f32[10,4,256]{2,1,0:T(4,128)S(1)}, f32[10,4,256]{2,1,0:T(4,128)}, u32[]{:S(2)}) copy-start(f32[10,4,256]{2,1,0:T(4,128)} %copy-done.8) | copy-start | bytes 122884
  145.5 4.5 %copy-start.10 = (pred[256,256]{1,0:T(8,128)(4,1)S(1)}, pred[256,256]{1,0:T(8,128)(4,1)}, u32[]{:S(2)}) copy-start(pred[256,256]{1,0:T(8,128)(4,1)} %iota_compare_fusion) | copy-start | bytes 196612
  145.5 4.5 %copy-start.11 = (f32[10,4,256]{2,1,0:T(4,128)S(1)}, f32[10,4,256]{2,1,0:T(4,128)}, u32[]{:S(2)}) copy-start(f32[10,4,256]{2,1,0:T(4,128)} %get-tuple-element.80) | copy-start | bytes 122884
  145.5 4.5 %copy-start.14 = (f32[10]{0:T(128)S(1)}, f32[10]{0:T(128)}, u32[]{:S(2)}) copy-start(f32[10]{0:T(128)} %param.12) | copy-start | bytes 124
Sparse Core Ops, SparseCore 0:
  156.5 60.5 all-gather.1
where the time goes:
time: 232 us; the launch traced here: 231 us
  waiting for transfers between devices  81 us (35%)
  starting transfers between devices  65.2 us (28%)
  other arithmetic  33.6 us (14%)
  matrix products  23.4 us (10%)
  local copies, waits for them, and re-layouts  14.2 us (6%)
  between operations  13.7 us (6%)
    ppermute x11, starting transfers between devices, shifted(): return lax.ppermute(value, 'seq', [(i, i + d) for i in range(peers - d)])  65.2 us
    all_gather x1, waiting for transfers between devices, on_device(): lax.all_gather(mixed_columns, 'grp', axis=0, tiled=True)  60.8 us
    ppermute x11, waiting for transfers between devices, shifted(): return lax.ppermute(value, 'seq', [(i, i + d) for i in range(peers - d)])  20.2 us
    add x4, other arithmetic, advance(): return (decay[:, None, None] * state + digest_record, state)  8.81 us
    select_n x5, other arithmetic, carry_in(): state = jnp.where(reached, decay[:, None, None] * state_r + state, state)  7.74 us
    dot_general x1, matrix products, on_device(): jnp.einsum('kt,kd->td', lax.all_gather(mixed_columns, 'grp', axis=0, tile...  7.17 us
    dynamic_update_slice x4, other arithmetic, on_device(): lax.scan(advance, zero_state, (block_decay.T, summaries))  6.89 us
    dot_general x1, matrix products, on_device(): jnp.einsum('hcjn,hpcj->chnp', weighted_terms, channels, preferred_element...  5.63 us
  transfers between devices with their start and end apart: 12, of which 7 were waited for; matrix products, arithmetic and copies ran while one was open for 4% of the time, Pallas kernels for 0%

commit v1 on v0

--- a/solution.py
+++ b/solution.py
@@ -6,6 +6,22 @@
 HP = 64
 N = 128
 GROUP = 256
+
+
+def ring_product(array, axis, dim, product):
+    size, index, rows = (lax.axis_size(axis), lax.axis_index(axis), array.shape[dim])
+    right = [(i, (i + 1) % size) for i in range(size)]
+    left = [(i, (i - 1) % size) for i in range(size)]
+    half = size // 2
+    from_left = from_right = array
+    so_far = product(array, index * rows)
+    for turn in range(1, half + 1):
+        from_left = lax.ppermute(from_left, axis, right)
+        if turn < size - half:
+            from_right = lax.ppermute(from_right, axis, left)
+            so_far = so_far + product(from_right, (index + turn) % size * rows)
+        so_far = so_far + product(from_left, (index - turn) % size * rows)
+    return so_far
 
 
 def carry_in(total_log, final_state):
@@ -80,11 +96,16 @@
     )
     mixed = inner + from_state * within + direct
     mixed_columns = mixed.astype(jnp.bfloat16).reshape(heads_here * HP, tokens_here)
-    result = jnp.einsum(
-        "kt,kd->td",
-        lax.all_gather(mixed_columns, "grp", axis=0, tiled=True),
-        out_weight,
-        preferred_element_type=jnp.float32,
+    result = ring_product(
+        mixed_columns,
+        "grp",
+        0,
+        lambda own_block, start: jnp.einsum(
+            "kt,kd->td",
+            own_block,
+            lax.dynamic_slice_in_dim(out_weight, start, own_block.shape[0], axis=0),
+            preferred_element_type=jnp.float32,
+        ),
     )
     return result.astype(jnp.bfloat16)
 

time: 232 us -> 225 us (0.970)
  the two profiles are of different devices: /device:TPU:1 before, /device:TPU:8 now
where the time goes in v1:
time: 225 us; the launch traced here: 224 us
  waiting for transfers between devices  113 us (50%)
  starting transfers between devices  37.4 us (17%)
  other arithmetic  29.2 us (13%)
  matrix products  29.2 us (13%)
  local copies, waits for them, and re-layouts  15.2 us (7%)
    ppermute x11, waiting for transfers between devices, shifted(): return lax.ppermute(value, 'seq', [(i, i + d) for i in range(peers - d)])  59.4 us
    ppermute x4, waiting for transfers between devices, ring_product(): from_left = lax.ppermute(from_left, axis, right)  53.1 us
    ppermute x11, starting transfers between devices, shifted(): return lax.ppermute(value, 'seq', [(i, i + d) for i in range(peers - d)])  30.6 us
    dot_general x8, matrix products, on_device(): jnp.einsum('kt,kd->td', own_block, lax.dynamic_slice_in_dim(out_weight, s...  12.9 us
    add x4, other arithmetic, advance(): return (decay[:, None, None] * state + digest_record, state)  8.81 us
    select_n x5, other arithmetic, carry_in(): state = jnp.where(reached, decay[:, None, None] * state_r + state, state)  7.77 us
    ppermute x3, starting transfers between devices, ring_product(): from_right = lax.ppermute(from_right, axis, left)  6.85 us
    dynamic_update_slice x4, other arithmetic, on_device(): lax.scan(advance, zero_state, (block_decay.T, summaries))  6.84 us
  transfers between devices with their start and end apart: 18, of which 12 were waited for; matrix products, arithmetic and copies ran while one was open for 7% of the time, Pallas kernels for 0%

profile of v1, /device:TPU:8, one launch (start us, length us, event | category | flops | bytes accessed | tf_op | source)
XLA Modules:
  0.0 224.1 jit_solution(11840203528060436300)
XLA Ops:
  2.8 2.3 %reduce-window.6 = f32[10,4,2,128]{3,0,1,2:T(8,128)S(1)} reduce-window(f32[10,4,2,128]{3,0,1,2:T(8,128)S(1)} %copy.30, f32[]{:T(128)} %constant.73.clone.1), window={size=1x1x1x128 pad=0_0x0_0x0_0x127_0}, to_apply=%region_0.0 | reduce-window | flops 1300480 | bytes 81924 | tf_op jit(solution)/shard_map/reduce-window
  7.0 3.8 %reshape.94 = bf16[10,64,4,256]{3,2,1,0:T(4,128)(2,1)} reshape(bf16[640,1024]{1,0:T(8,128)(2,1)} %param.9) | data formatting | bytes 2621440 | tf_op jit(solution)/shard_map/reshape | solution.py:52
  11.7 5.7 %fusion.8 = f32[4,10,128,64]{3,2,1,0:T(8,128)} fusion(f32[10,4,256]{2,0,1:T(8,128)} %copy.35, f32[4,256,128]{2,1,0:T(8,128)} %convert_element_type.24, bf16[10,64,4,256]{3,2,1,0:T(4,128)(2,1)} %reshape.94), kind=kOutput, calls=%fused_computation.13 | convolution fusion | flops 170393600 | bytes 3186688 | tf_op jit(solution)/shard_map/hcjn,hpcj->chnp/dot_general | solution.py:75
  17.3 15.7 %while.13 = (s32[]{:T(128)}, f32[10,128,64]{2,1,0:T(8,128)}, f32[4,10,128,64]{3,2,1,0:T(8,128)}, f32[4,10]{1,0:T(4,128)S(1)}, f32[4,10,128,64]{3,2,1,0:T(8,128)}, /*index=5*/s32[]{:T(128)}, s32[]{:T(128)}) while((s32[]{:T(128)}, f32[10,128,64]{2,1,0:T(8,128)}, f32[4,10,128,64]{3,2,1,0:T(8,128)}, f32[4,10]{1,0:T(4,128)S(1)}, ...), condition=%wide.region_3.4_spmd.clone, body=%wide.region_2.3_spmd.clone.sunk | while | flops 327683 | bytes 2294488 | solution.py:85
  18.2 2.1 bitcast_add_fusion.2
  20.3 2.0 bitcast_dynamic-update-slice_fusion.2
  22.3 2.3 %bitcast_add_fusion.2 = f32[10,128,64]{2,1,0:T(8,128)} fusion(f32[4,10,128,64]{3,2,1,0:T(8,128)} %get-tuple-element.131, s32[]{:T(128)} %get-tuple-element.120, f32[10,128,64]{2,1,0:T(8,128)} %get-tuple-element.121, f32[10]{0:T(128)S(1)} %fusion.58, pred[]{:T(512)S(6)} %compare.10), kind=kLoop, calls=%fused_computation.1.clone.1 | loop fusion | flops 245760 | bytes 983085 | tf_op jit(solution)/shard_map/while/body/eval_jaxpr/add | solution.py:82
  24.5 2.0 bitcast_dynamic-update-slice_fusion.2
  26.5 2.3 %bitcast_add_fusion.2 = f32[10,128,64]{2,1,0:T(8,128)} fusion(f32[4,10,128,64]{3,2,1,0:T(8,128)} %get-tuple-element.131, s32[]{:T(128)} %get-tuple-element.120, f32[10,128,64]{2,1,0:T(8,128)} %get-tuple-element.121, f32[10]{0:T(128)S(1)} %fusion.58, pred[]{:T(512)S(6)} %compare.10), kind=kLoop, calls=%fused_computation.1.clone.1 | loop fusion | flops 245760 | bytes 983085 | tf_op jit(solution)/shard_map/while/body/eval_jaxpr/add | solution.py:82
  28.8 2.0 bitcast_dynamic-update-slice_fusion.2
  30.8 2.3 %bitcast_add_fusion.2 = f32[10,128,64]{2,1,0:T(8,128)} fusion(f32[4,10,128,64]{3,2,1,0:T(8,128)} %get-tuple-element.131, s32[]{:T(128)} %get-tuple-element.120, f32[10,128,64]{2,1,0:T(8,128)} %get-tuple-element.121, f32[10]{0:T(128)S(1)} %fusion.58, pred[]{:T(512)S(6)} %compare.10), kind=kLoop, calls=%fused_computation.1.clone.1 | loop fusion | flops 245760 | bytes 983085 | tf_op jit(solution)/shard_map/while/body/eval_jaxpr/add | solution.py:82
  33.0 2.0 copy.39
  35.0 3.8 %collective-permute-start.5 = (f32[10,128,64]{1,2,0:T(8,128)}, f32[10,128,64]{1,2,0:T(8,128)}, u32[]{:S(2)}, u32[]{:S(2)}) collective-permute-start(f32[10,128,64]{1,2,0:T(8,128)} %copy.39), channel_id=1, source_target_pairs={{0,8},{8,16},{16,24},{24,32},{32,40},{40,48},{48,56},{56,64},{64,7... | collective-permute-start | bytes 983048 | tf_op jit(solution)/shard_map/ppermute | solution.py:31
  38.9 11.8 %collective-permute-done.5 = f32[10,128,64]{1,2,0:T(8,128)} collective-permute-done((f32[10,128,64]{1,2,0:T(8,128)}, f32[10,128,64]{1,2,0:T(8,128)}, u32[]{:S(2)}, u32[]{:S(2)}) %collective-permute-start.5) | collective-permute-done | bytes 327712 | tf_op jit(solution)/shard_map/ppermute | solution.py:31
  50.7 1.9 collective-permute-start.6
  52.6 1.9 collective-permute-start
  54.6 9.3 %collective-permute-done = f32[10]{0:T(128)S(1)} collective-permute-done((f32[10]{0:T(128)S(1)}, f32[10]{0:T(128)S(1)}, u32[]{:S(2)}, u32[]{:S(2)}) %collective-permute-start) | collective-permute-done | bytes 72 | tf_op jit(solution)/shard_map/ppermute | solution.py:31
  63.9 1.9 add_select_fusion.4
  65.8 1.9 collective-permute-start.7
  67.7 2.5 %collective-permute-start.1 = (f32[10]{0:T(128)S(1)}, f32[10]{0:T(128)S(1)}, u32[]{:S(2)}, u32[]{:S(2)}) collective-permute-start(f32[10]{0:T(128)S(1)} %broadcast_select_fusion.1), channel_id=1, source_target_pairs={{0,8},{8,16},{16,24},{24,32},{32,40},{40,48},{48,56},{56,64},{64,7... | collective-permute-start | bytes 128 | tf_op jit(solution)/shard_map/ppermute | solution.py:31
  70.3 10.6 %collective-permute-done.1 = f32[10]{0:T(128)S(1)} collective-permute-done((f32[10]{0:T(128)S(1)}, f32[10]{0:T(128)S(1)}, u32[]{:S(2)}, u32[]{:S(2)}) %collective-permute-start.1) | collective-permute-done | bytes 72 | tf_op jit(solution)/shard_map/ppermute | solution.py:31
  80.9 3.3 %collective-permute-done.7 = f32[10,128,64]{1,2,0:T(8,128)} collective-permute-done((f32[10,128,64]{1,2,0:T(8,128)}, f32[10,128,64]{1,2,0:T(8,128)}, u32[]{:S(2)}, u32[]{:S(2)}) %collective-permute-start.7) | collective-permute-done | bytes 327712 | tf_op jit(solution)/shard_map/ppermute | solution.py:31
  86.0 4.2 %collective-permute-start.8 = (f32[10,128,64]{1,2,0:T(8,128)}, f32[10,128,64]{1,2,0:T(8,128)}, u32[]{:S(2)}, u32[]{:S(2)}) collective-permute-start(f32[10,128,64]{1,2,0:T(8,128)} %add_select_fusion.3), channel_id=1, source_target_pairs={{0,32},{8,40},{16,48},{24,56},{32,64},{40,72},{48,80},{56,88},{64,... | collective-permute-start | bytes 983048 | tf_op jit(solution)/shard_map/ppermute | solution.py:31
  90.2 2.2 fusion.44
  93.6 2.6 %collective-permute-start.2 = (f32[10]{0:T(128)S(1)}, f32[10]{0:T(128)S(1)}, u32[]{:S(2)}, u32[]{:S(2)}) collective-permute-start(f32[10]{0:T(128)S(1)} %broadcast_select_fusion), channel_id=1, source_target_pairs={{0,16},{8,24},{16,32},{24,40},{32,48},{40,56},{48,64},{56,72},{64,... | collective-permute-start | bytes 128 | tf_op jit(solution)/shard_map/ppermute | solution.py:31
  96.2 7.8 %collective-permute-done.2 = f32[10]{0:T(128)S(1)} collective-permute-done((f32[10]{0:T(128)S(1)}, f32[10]{0:T(128)S(1)}, u32[]{:S(2)}, u32[]{:S(2)}) %collective-permute-start.2) | collective-permute-done | bytes 72 | tf_op jit(solution)/shard_map/ppermute | solution.py:31
  104.0 3.6 %collective-permute-done.8 = f32[10,128,64]{1,2,0:T(8,128)} collective-permute-done((f32[10,128,64]{1,2,0:T(8,128)}, f32[10,128,64]{1,2,0:T(8,128)}, u32[]{:S(2)}, u32[]{:S(2)}) %collective-permute-start.8) | collective-permute-done | bytes 327712 | tf_op jit(solution)/shard_map/ppermute | solution.py:31
  109.5 3.5 %collective-permute-start.9 = (f32[10,128,64]{1,2,0:T(8,128)}, f32[10,128,64]{1,2,0:T(8,128)}, u32[]{:S(2)}, u32[]{:S(2)}) collective-permute-start(f32[10,128,64]{1,2,0:T(8,128)} %add_select_fusion.2), channel_id=1, source_target_pairs={{0,64},{8,72},{16,80},{24,88},{32,96},{40,104},{48,112},{56,120},{... | collective-permute-start | bytes 983048 | tf_op jit(solution)/shard_map/ppermute | solution.py:31
  113.1 3.3 %collective-permute-start.3 = (f32[10]{0:T(128)S(1)}, f32[10]{0:T(128)S(1)}, u32[]{:S(2)}, u32[]{:S(2)}) collective-permute-start(f32[10]{0:T(128)S(1)} %broadcast_select_fusion.2), channel_id=1, source_target_pairs={{0,32},{8,40},{16,48},{24,56},{32,64},{40,72},{48,80},{56,88},{64,... | collective-permute-start | bytes 128 | tf_op jit(solution)/shard_map/ppermute | solution.py:31
  116.4 6.9 %collective-permute-done.3 = f32[10]{0:T(128)S(1)} collective-permute-done((f32[10]{0:T(128)S(1)}, f32[10]{0:T(128)S(1)}, u32[]{:S(2)}, u32[]{:S(2)}) %collective-permute-start.3) | collective-permute-done | bytes 72 | tf_op jit(solution)/shard_map/ppermute | solution.py:31
  124.6 2.4 %collective-permute-start.10 = (f32[10,128,64]{1,2,0:T(8,128)S(1)}, f32[10,128,64]{1,2,0:T(8,128)S(1)}, u32[]{:S(2)}, u32[]{:S(2)}) collective-permute-start(f32[10,128,64]{1,2,0:T(8,128)S(1)} %add_select_fusion.1), channel_id=1, source_target_pairs={{0,128},{8,136},{16,144},{24,152},{32,160},{40,168},{48,176},{56,1... | collective-permute-start | bytes 983048 | tf_op jit(solution)/shard_map/ppermute | solution.py:31
  127.6 2.5 %collective-permute-start.4 = (f32[10]{0:T(128)S(1)}, f32[10]{0:T(128)S(1)}, u32[]{:S(2)}, u32[]{:S(2)}) collective-permute-start(f32[10]{0:T(128)S(1)} %broadcast_select_fusion.3), channel_id=1, source_target_pairs={{0,64},{8,72},{16,80},{24,88},{32,96},{40,104},{48,112},{56,120},{... | collective-permute-start | bytes 128 | tf_op jit(solution)/shard_map/ppermute | solution.py:31
  130.1 6.1 %collective-permute-done.4 = f32[10]{0:T(128)S(1)} collective-permute-done((f32[10]{0:T(128)S(1)}, f32[10]{0:T(128)S(1)}, u32[]{:S(2)}, u32[]{:S(2)}) %collective-permute-start.4) | collective-permute-done | bytes 72 | tf_op jit(solution)/shard_map/ppermute | solution.py:31
  137.1 2.0 copy.40
  139.2 4.4 %fusion.12 = f32[4,10,64,256]{3,2,0,1:T(8,128)S(1)} fusion(bf16[4,256,128,1]{2,1,0,3:T(8,128)(2,1)S(1)} %bitcast.54, f32[4,10,128,64]{3,2,1,0:T(8,128)} %get-tuple-element.33, f32[10,128,64]{2,1,0:T(8,128)} %copy.40, f32[4,10]{1,0:T(4,128)S(1)} %copy.38), kind=kOutput, calls=%fused_computation.18 | convolution fusion | flops 1007288320 | bytes 4522144 | tf_op jit(solution)/shard_map/cin,chnp->hpci/dot_general | solution.py:94
  143.6 4.0 %fusion.11 = bf16[10,64,4,256]{3,1,2,0:T(8,128)(2,1)S(1)} fusion(f32[4,10,64,256]{3,2,0,1:T(8,128)S(1)} %fusion.12, f32[10,4,256]{2,1,0:T(4,128)S(1)} %copy-done.12, f32[10,4,256]{2,1,0:T(4,128)S(1)} %copy-done.10, f32[4,256,256]{2,1,0:T(8,128)S(1)} %copy-done.5, pred[256,256]{1,0:T(8,128)(4,1)S(1)} %copy-done.13, ...), kind=kOutput, calls=%fused_computation.17 | convolution fusion | flops 355205120 | bytes 6479912 | tf_op jit(solution)/shard_map/hcij,hpcj->hpci/dot_general | solution.py:70
  150.0 1.9 collective-permute-start.11
  151.9 15.3 %collective-permute-done.12 = bf16[640,1024]{1,0:T(8,128)(2,1)S(1)} collective-permute-done((bf16[640,1024]{1,0:T(8,128)(2,1)S(1)}, bf16[640,1024]{1,0:T(8,128)(2,1)S(1)}, u32[]{:S(2)}, u32[]{:S(2)}) %collective-permute-start.12) | collective-permute-done | bytes 1310752 | tf_op jit(solution)/shard_map/ppermute | solution.py:19
  168.3 2.0 collective-permute-start.13
  170.3 15.3 %collective-permute-done.14 = bf16[640,1024]{1,0:T(8,128)(2,1)} collective-permute-done((bf16[640,1024]{1,0:T(8,128)(2,1)S(1)}, bf16[640,1024]{1,0:T(8,128)(2,1)}, u32[]{:S(2)}, u32[]{:S(2)}) %collective-permute-start.14) | collective-permute-done | bytes 1310752 | tf_op jit(solution)/shard_map/ppermute | solution.py:19
  185.5 2.0 fusion.30
  187.6 3.0 %collective-permute-start.15 = (bf16[640,1024]{1,0:T(8,128)(2,1)}, bf16[640,1024]{1,0:T(8,128)(2,1)S(1)}, u32[]{:S(2)}, u32[]{:S(2)}) collective-permute-start(bf16[640,1024]{1,0:T(8,128)(2,1)} %collective-permute-done.13), channel_id=1, source_target_pairs={{0,7},{1,0},{2,1},{3,2},{4,3},{5,4},{6,5},{7,6},{8,15},{9,8},{10,9... | collective-permute-start | bytes 3932168 | tf_op jit(solution)/shard_map/ppermute | solution.py:21
  190.5 2.0 convolution_add_fusion.4
  192.5 11.6 %collective-permute-done.16 = bf16[640,1024]{1,0:T(8,128)(2,1)} collective-permute-done((bf16[640,1024]{1,0:T(8,128)(2,1)}, bf16[640,1024]{1,0:T(8,128)(2,1)}, u32[]{:S(2)}, u32[]{:S(2)}) %collective-permute-start.16) | collective-permute-done | bytes 1310752 | tf_op jit(solution)/shard_map/ppermute | solution.py:19
  204.8 2.0 fusion.25
  206.8 2.0 fusion.16
  208.8 2.0 fusion.22
  211.6 11.0 %collective-permute-done.17 = bf16[640,1024]{1,0:T(8,128)(2,1)S(1)} collective-permute-done((bf16[640,1024]{1,0:T(8,128)(2,1)}, bf16[640,1024]{1,0:T(8,128)(2,1)S(1)}, u32[]{:S(2)}, u32[]{:S(2)}) %collective-permute-start.17) | collective-permute-done | bytes 1310752 | tf_op jit(solution)/shard_map/ppermute | solution.py:19
  (89 shorter events, 20.6 us)
Async XLA Ops:
  0.0 185.5 %copy-start = (bf16[5120,320]{0,1:T(8,128)(2,1)S(1)}, bf16[5120,320]{0,1:T(8,128)(2,1)}, u32[]{:S(2)}) copy-start(bf16[5120,320]{0,1:T(8,128)(2,1)} %param.15) | copy-start | bytes 9830404
  1.0 5.4 %copy-start.11 = (f32[10,4,256]{2,1,0:T(4,128)}, f32[10,4,256]{2,1,0:T(4,128)S(1)}, u32[]{:S(2)}) copy-start(f32[10,4,256]{2,1,0:T(4,128)S(1)} %mul.165) | copy-start | bytes 122884
  2.1 0.6 copy-start.8
  5.4 0.9 copy-start.9
  7.0 3.8 %copy-start.6 = (bf16[1024,128]{1,0:T(8,128)(2,1)S(1)}, bf16[1024,128]{1,0:T(8,128)(2,1)}, u32[]{:S(2)}) copy-start(bf16[1024,128]{1,0:T(8,128)(2,1)} %param.13) | copy-start | bytes 786436
  35.0 15.7 %collective-permute-start.5 = (f32[10,128,64]{1,2,0:T(8,128)}, f32[10,128,64]{1,2,0:T(8,128)}, u32[]{:S(2)}, u32[]{:S(2)}) collective-permute-start(f32[10,128,64]{1,2,0:T(8,128)} %copy.39), channel_id=1, source_target_pairs={{0,8},{8,16},{16,24},{24,32},{32,40},{40,48},{48,56},{56,64},{64,7... | collective-permute-start | bytes 983048 | tf_op jit(solution)/shard_map/ppermute | solution.py:31
  50.7 13.2 %collective-permute-start.6 = (f32[10,128,64]{1,2,0:T(8,128)}, f32[10,128,64]{1,2,0:T(8,128)}, u32[]{:S(2)}, u32[]{:S(2)}) collective-permute-start(f32[10,128,64]{1,2,0:T(8,128)} %collective-permute-done.5), channel_id=1, source_target_pairs={{0,8},{8,16},{16,24},{24,32},{32,40},{40,48},{48,56},{56,64},{64,7... | collective-permute-start | bytes 983048 | tf_op jit(solution)/shard_map/ppermute | solution.py:31
  52.6 11.3 %collective-permute-start = (f32[10]{0:T(128)S(1)}, f32[10]{0:T(128)S(1)}, u32[]{:S(2)}, u32[]{:S(2)}) collective-permute-start(f32[10]{0:T(128)S(1)} %negate_exponential_fusion), channel_id=1, source_target_pairs={{0,8},{8,16},{16,24},{24,32},{32,40},{40,48},{48,56},{56,64},{64,7... | collective-permute-start | bytes 128 | tf_op jit(solution)/shard_map/ppermute | solution.py:31
  65.8 18.3 %collective-permute-start.7 = (f32[10,128,64]{1,2,0:T(8,128)}, f32[10,128,64]{1,2,0:T(8,128)}, u32[]{:S(2)}, u32[]{:S(2)}) collective-permute-start(f32[10,128,64]{1,2,0:T(8,128)} %add_select_fusion.4), channel_id=1, source_target_pairs={{0,16},{8,24},{16,32},{24,40},{32,48},{40,56},{48,64},{56,72},{64,... | collective-permute-start | bytes 983048 | tf_op jit(solution)/shard_map/ppermute | solution.py:31
  67.7 13.1 %collective-permute-start.1 = (f32[10]{0:T(128)S(1)}, f32[10]{0:T(128)S(1)}, u32[]{:S(2)}, u32[]{:S(2)}) collective-permute-start(f32[10]{0:T(128)S(1)} %broadcast_select_fusion.1), channel_id=1, source_target_pairs={{0,8},{8,16},{16,24},{24,32},{32,40},{40,48},{48,56},{56,64},{64,7... | collective-permute-start | bytes 128 | tf_op jit(solution)/shard_map/ppermute | solution.py:31
  86.0 21.5 %collective-permute-start.8 = (f32[10,128,64]{1,2,0:T(8,128)}, f32[10,128,64]{1,2,0:T(8,128)}, u32[]{:S(2)}, u32[]{:S(2)}) collective-permute-start(f32[10,128,64]{1,2,0:T(8,128)} %add_select_fusion.3), channel_id=1, source_target_pairs={{0,32},{8,40},{16,48},{24,56},{32,64},{40,72},{48,80},{56,88},{64,... | collective-permute-start | bytes 983048 | tf_op jit(solution)/shard_map/ppermute | solution.py:31
  93.6 10.4 %collective-permute-start.2 = (f32[10]{0:T(128)S(1)}, f32[10]{0:T(128)S(1)}, u32[]{:S(2)}, u32[]{:S(2)}) collective-permute-start(f32[10]{0:T(128)S(1)} %broadcast_select_fusion), channel_id=1, source_target_pairs={{0,16},{8,24},{16,32},{24,40},{32,48},{40,56},{48,64},{56,72},{64,... | collective-permute-start | bytes 128 | tf_op jit(solution)/shard_map/ppermute | solution.py:31
  109.5 13.9 %collective-permute-start.9 = (f32[10,128,64]{1,2,0:T(8,128)}, f32[10,128,64]{1,2,0:T(8,128)}, u32[]{:S(2)}, u32[]{:S(2)}) collective-permute-start(f32[10,128,64]{1,2,0:T(8,128)} %add_select_fusion.2), channel_id=1, source_target_pairs={{0,64},{8,72},{16,80},{24,88},{32,96},{40,104},{48,112},{56,120},{... | collective-permute-start | bytes 983048 | tf_op jit(solution)/shard_map/ppermute | solution.py:31
  113.1 10.2 %collective-permute-start.3 = (f32[10]{0:T(128)S(1)}, f32[10]{0:T(128)S(1)}, u32[]{:S(2)}, u32[]{:S(2)}) collective-permute-start(f32[10]{0:T(128)S(1)} %broadcast_select_fusion.2), channel_id=1, source_target_pairs={{0,32},{8,40},{16,48},{24,56},{32,64},{40,72},{48,80},{56,88},{64,... | collective-permute-start | bytes 128 | tf_op jit(solution)/shard_map/ppermute | solution.py:31
  123.3 15.8 %copy-start.7 = (bf16[1024,128]{1,0:T(8,128)(2,1)S(1)}, bf16[1024,128]{1,0:T(8,128)(2,1)}, u32[]{:S(2)}) copy-start(bf16[1024,128]{1,0:T(8,128)(2,1)} %param.14) | copy-start | bytes 786436
  124.6 11.7 %collective-permute-start.10 = (f32[10,128,64]{1,2,0:T(8,128)S(1)}, f32[10,128,64]{1,2,0:T(8,128)S(1)}, u32[]{:S(2)}, u32[]{:S(2)}) collective-permute-start(f32[10,128,64]{1,2,0:T(8,128)S(1)} %add_select_fusion.1), channel_id=1, source_target_pairs={{0,128},{8,136},{16,144},{24,152},{32,160},{40,168},{48,176},{56,1... | collective-permute-start | bytes 983048 | tf_op jit(solution)/shard_map/ppermute | solution.py:31
  127.6 8.6 %collective-permute-start.4 = (f32[10]{0:T(128)S(1)}, f32[10]{0:T(128)S(1)}, u32[]{:S(2)}, u32[]{:S(2)}) collective-permute-start(f32[10]{0:T(128)S(1)} %broadcast_select_fusion.3), channel_id=1, source_target_pairs={{0,64},{8,72},{16,80},{24,88},{32,96},{40,104},{48,112},{56,120},{... | collective-permute-start | bytes 128 | tf_op jit(solution)/shard_map/ppermute | solution.py:31
  139.1 4.4 %copy-start.4 = (bf16[10,64,4,256]{3,2,1,0:T(4,128)(2,1)S(1)}, bf16[10,64,4,256]{3,2,1,0:T(4,128)(2,1)}, u32[]{:S(2)}) copy-start(bf16[10,64,4,256]{3,2,1,0:T(4,128)(2,1)} %reshape.94) | copy-start | bytes 3932164
  139.1 4.4 %copy-start.5 = (f32[4,256,256]{2,1,0:T(8,128)S(1)}, f32[4,256,256]{2,1,0:T(8,128)}, u32[]{:S(2)}) copy-start(f32[4,256,256]{2,1,0:T(8,128)} %fusion.44) | copy-start | bytes 3145732
  139.1 4.5 %copy-start.10 = (f32[10,4,256]{2,1,0:T(4,128)S(1)}, f32[10,4,256]{2,1,0:T(4,128)}, u32[]{:S(2)}) copy-start(f32[10,4,256]{2,1,0:T(4,128)} %copy-done.9) | copy-start | bytes 122884
  139.1 4.5 %copy-start.12 = (f32[10,4,256]{2,1,0:T(4,128)S(1)}, f32[10,4,256]{2,1,0:T(4,128)}, u32[]{:S(2)}) copy-start(f32[10,4,256]{2,1,0:T(4,128)} %copy-done.11) | copy-start | bytes 122884
  139.1 4.5 %copy-start.13 = (pred[256,256]{1,0:T(8,128)(4,1)S(1)}, pred[256,256]{1,0:T(8,128)(4,1)}, u32[]{:S(2)}) copy-start(pred[256,256]{1,0:T(8,128)(4,1)} %iota_compare_fusion) | copy-start | bytes 196612
  139.1 4.5 %copy-start.14 = (f32[10,4,256]{2,1,0:T(4,128)S(1)}, f32[10,4,256]{2,1,0:T(4,128)}, u32[]{:S(2)}) copy-start(f32[10,4,256]{2,1,0:T(4,128)} %get-tuple-element.80) | copy-start | bytes 122884
  139.1 4.5 %copy-start.15 = (f32[10]{0:T(128)S(1)}, f32[10]{0:T(128)}, u32[]{:S(2)}) copy-start(f32[10]{0:T(128)} %param.12) | copy-start | bytes 124
  148.9 1.1 copy-start.1
  148.9 18.3 %collective-permute-start.12 = (bf16[640,1024]{1,0:T(8,128)(2,1)S(1)}, bf16[640,1024]{1,0:T(8,128)(2,1)S(1)}, u32[]{:S(2)}, u32[]{:S(2)}) collective-permute-start(bf16[640,1024]{1,0:T(8,128)(2,1)S(1)} %bitcast.47), channel_id=1, source_target_pairs={{0,1},{1,2},{2,3},{3,4},{4,5},{5,6},{6,7},{7,0},{8,9},{9,10},{10,1... | collective-permute-start | bytes 3932168 | tf_op jit(solution)/shard_map/ppermute | solution.py:19
  150.0 17.2 %collective-permute-start.11 = (bf16[640,1024]{1,0:T(8,128)(2,1)S(1)}, bf16[640,1024]{1,0:T(8,128)(2,1)}, u32[]{:S(2)}, u32[]{:S(2)}) collective-permute-start(bf16[640,1024]{1,0:T(8,128)(2,1)S(1)} %bitcast.48), channel_id=1, source_target_pairs={{0,7},{1,0},{2,1},{3,2},{4,3},{5,4},{6,5},{7,6},{8,15},{9,8},{10,9... | collective-permute-start | bytes 3932168 | tf_op jit(solution)/shard_map/ppermute | solution.py:21
  167.2 1.1 copy-start.2
  167.2 18.3 %collective-permute-start.14 = (bf16[640,1024]{1,0:T(8,128)(2,1)S(1)}, bf16[640,1024]{1,0:T(8,128)(2,1)}, u32[]{:S(2)}, u32[]{:S(2)}) collective-permute-start(bf16[640,1024]{1,0:T(8,128)(2,1)S(1)} %collective-permute-done.12), channel_id=1, source_target_pairs={{0,1},{1,2},{2,3},{3,4},{4,5},{5,6},{6,7},{7,0},{8,9},{9,10},{10,1... | collective-permute-start | bytes 3932168 | tf_op jit(solution)/shard_map/ppermute | solution.py:19
  168.3 19.3 %collective-permute-start.13 = (bf16[640,1024]{1,0:T(8,128)(2,1)}, bf16[640,1024]{1,0:T(8,128)(2,1)}, u32[]{:S(2)}, u32[]{:S(2)}) collective-permute-start(bf16[640,1024]{1,0:T(8,128)(2,1)} %collective-permute-done.11), channel_id=1, source_target_pairs={{0,7},{1,0},{2,1},{3,2},{4,3},{5,4},{6,5},{7,6},{8,15},{9,8},{10,9... | collective-permute-start | bytes 3932168 | tf_op jit(solution)/shard_map/ppermute | solution.py:21
  185.5 18.6 %collective-permute-start.16 = (bf16[640,1024]{1,0:T(8,128)(2,1)}, bf16[640,1024]{1,0:T(8,128)(2,1)}, u32[]{:S(2)}, u32[]{:S(2)}) collective-permute-start(bf16[640,1024]{1,0:T(8,128)(2,1)} %collective-permute-done.14), channel_id=1, source_target_pairs={{0,1},{1,2},{2,3},{3,4},{4,5},{5,6},{6,7},{7,0},{8,9},{9,10},{10,1... | collective-permute-start | bytes 3932168 | tf_op jit(solution)/shard_map/ppermute | solution.py:19
  187.5 16.6 %copy-start.3 = (bf16[640,1024]{1,0:T(8,128)(2,1)S(1)}, bf16[640,1024]{1,0:T(8,128)(2,1)}, u32[]{:S(2)}) copy-start(bf16[640,1024]{1,0:T(8,128)(2,1)} %copy-done.2) | copy-start | bytes 3932164
  187.6 23.3 %collective-permute-start.15 = (bf16[640,1024]{1,0:T(8,128)(2,1)}, bf16[640,1024]{1,0:T(8,128)(2,1)S(1)}, u32[]{:S(2)}, u32[]{:S(2)}) collective-permute-start(bf16[640,1024]{1,0:T(8,128)(2,1)} %collective-permute-done.13), channel_id=1, source_target_pairs={{0,7},{1,0},{2,1},{3,2},{4,3},{5,4},{6,5},{7,6},{8,15},{9,8},{10,9... | collective-permute-start | bytes 3932168 | tf_op jit(solution)/shard_map/ppermute | solution.py:21
  204.1 18.5 %collective-permute-start.17 = (bf16[640,1024]{1,0:T(8,128)(2,1)}, bf16[640,1024]{1,0:T(8,128)(2,1)S(1)}, u32[]{:S(2)}, u32[]{:S(2)}) collective-permute-start(bf16[640,1024]{1,0:T(8,128)(2,1)} %collective-permute-done.16), channel_id=1, source_target_pairs={{0,1},{1,2},{2,3},{3,4},{4,5},{5,6},{6,7},{7,0},{8,9},{9,10},{10,1... | collective-permute-start | bytes 3932168 | tf_op jit(solution)/shard_map/ppermute | solution.py:19
